TPU v7x, 32 devices: a whole 2x2x4 slice. The times are simulated.
32 devices in a mesh: lon: 4 (over y, x), lat: 8 (over z, core).
Axes of the slice: x: 2, y: 2, z: 4, core: 2. Of those that a mesh axis runs over, the one named last changes fastest.
Arguments:
- state_adjoint: float32 [4, 4, 512, 1024], P(None, None, 'lat', 'lon'), may hold values from -6 to 6
- east_velocity: float32 [4, 512, 1024], P(None, 'lat', 'lon'), may hold values from -1.2 to 1.2
- north_velocity: float32 [4, 512, 1024], P(None, 'lat', 'lon'), may hold values from -1.2 to 1.2
- ocean_mask: int32 [4, 512, 1024], P(None, 'lat', 'lon'), may hold values 0 or 1
- partner: int32 [1024], P('lon'), may hold values from 0 to 1023, as said below
Outputs:
- sensitivity: float32 [4, 4, 512, 1024], P(None, None, 'lat', 'lon')
Inputs may be any that keep to these rules, and one draw needn't show every extreme that they name: partner[i] = (c - i) mod 1024 with one c for all columns, 1023 <= c <= 1278; hence partner[partner[i]] = i.
All inputs are finite; a program needn't handle non-finite values. No bound on the sum of `ocean_mask` on one device may be relied on, other than what follows from the above.
Results may differ from a plain program's by a relative error of at most 0.00002.
Values sent between devices are 32-bit elements; how exact they have to be, the bound alone decides.
No kernel may reach another device: no remote copies, remote signals or barrier semaphores. Data moves between devices by JAX's collectives and lax.ppermute only.
A program may use at most 64 MiB of HBM per device.

v0:
```python
import jax
import jax.numpy as jnp
from jax import lax
from jax.sharding import PartitionSpec as P

STEPS = 2


def shifted(shard, axis, by):
    count = lax.axis_size(axis)
    return lax.ppermute(shard, axis, [(i, (i + by) % count) for i in range(count)])


def shifted_2(shard, axis, by):
    count = lax.axis_size(axis)
    pairs = [(i, i + by) for i in range(count) if 0 <= i + by < count]
    return lax.ppermute(shard, axis, pairs)


def with_halo(block, sides, width, periodic):
    for axis, dim in sides:
        count = lax.axis_size(axis)
        forward = [(i, i + 1) for i in range(count - 1)]
        if periodic:
            forward.append((count - 1, 0))
        backward = [(target, source) for source, target in forward]
        low = lax.ppermute(
            lax.slice_in_dim(block, block.shape[dim] - width, None, axis=dim), axis, forward
        )
        high = lax.ppermute(lax.slice_in_dim(block, 0, width, axis=dim), axis, backward)
        block = jnp.concatenate([low, block, high], axis=dim)
    return block


def per_device(state_adjoint, east_velocity, north_velocity, ocean_mask, partner):
    wet_cells = ocean_mask.astype(jnp.float32)
    fold_signs = jnp.array([1.0, 1.0, -1.0, -1.0], dtype=jnp.float32).reshape(4, 1, 1)
    lat_place = lax.axis_index("lat")
    lat_count = lax.axis_size("lat")
    is_top = (lat_place == lat_count - 1).astype(jnp.float32)
    speed_west_edge = shifted(east_velocity[:, :, -1:], "lon", 1)
    speed_south_edge = shifted_2(north_velocity[:, -1:, :], "lat", 1)
    west_speed = jnp.concatenate([speed_west_edge, east_velocity[:, :, :-1]], axis=2)
    south_speed = jnp.concatenate([speed_south_edge, north_velocity[:, :-1, :]], axis=1)
    fold_weight = 1.0 + north_velocity[:, -1, :]
    current = state_adjoint
    for iteration in range(STEPS):
        masked = wet_cells * current
        lon_padded = with_halo(masked, (("lon", 3),), 1, True)
        lat_padded = with_halo(masked, (("lat", 2),), 1, False)
        west_rim = lon_padded[:, :, :, 0]
        east_rim = lon_padded[:, :, :, -1]
        south_rim = lat_padded[:, :, 0, :]
        north_rim = lat_padded[:, :, -1, :]
        east_adj = jnp.concatenate([masked[..., 1:], east_rim[..., None]], axis=3)
        west_adj = jnp.concatenate([west_rim[..., None], masked[..., :-1]], axis=3)
        north_adj = jnp.concatenate([masked[:, :, 1:, :], north_rim[:, :, None, :]], axis=2)
        south_adj = jnp.concatenate([south_rim[:, :, None, :], masked[:, :, :-1, :]], axis=2)
        transport = (
            0.5 * east_velocity * (east_adj - masked)
            + 0.5 * west_speed * (masked - west_adj)
            + 0.5 * north_velocity * (north_adj - masked)
            + 0.5 * south_speed * (masked - south_adj)
        )
        fold_flux = fold_weight * masked[:, :, -1, :]
        whole_row = lax.all_gather(fold_flux, "lon", axis=2, tiled=True)
        picked = jnp.take(whole_row, partner, axis=2)
        folded = 0.5 * fold_signs * picked
        total = masked + transport
        total = total.at[:, :, -1, :].add(is_top * folded)
        current = wet_cells * total
    return current


def solution(mesh):
    placed = (
        P(None, None, "lat", "lon"),
        P(None, "lat", "lon"),
        P(None, "lat", "lon"),
        P(None, "lat", "lon"),
        P("lon"),
    )
    return jax.shard_map(
        per_device,
        mesh=mesh,
        in_specs=placed,
        out_specs=P(None, None, "lat", "lon"),
        check_vma=False,
    )
```

profile of v0, /device:TPU:10, one launch (start us, length us, event | category | flops | bytes accessed | tf_op | source)
XLA Modules:
  0.0 109.1 jit_solution(16763126374377405692)
XLA Ops:
  0.0 0.8 broadcast_add_fusion
  0.8 1.9 %collective-permute-start.4 = (f32[4,1,256]{2,1,0:T(1,128)S(1)}, f32[4,1,256]{2,1,0:T(1,128)S(1)}, u32[]{:S(2)}, u32[]{:S(2)}) collective-permute-start(f32[4,1,256]{2,1,0:T(1,128)S(1)} %get-tuple-element.47), channel_id=1, source_target_pairs={{0,1},{1,2},{2,3},{3,4},{4,5},{5,6},{6,7},{8,9},{9,10},{10,11},{11... | collective-permute-start | bytes 12296 | tf_op jit(solution)/shard_map/ppermute | solution.py:17
  2.7 1.7 %slice.119 = f32[4,64,1]{2,1,0:T(8,128)} slice(f32[4,64,256]{2,1,0:T(8,128)} %param.13), slice={[0:4], [0:64], [255:256]} | slice | bytes 2048 | tf_op jit(solution)/shard_map/slice | solution.py:41
  4.3 1.5 %collective-permute-start.1 = (f32[4,64,1]{2,1,0:T(8,128)}, f32[4,64,1]{2,1,0:T(8,128)}, u32[]{:S(2)}, u32[]{:S(2)}) collective-permute-start(f32[4,64,1]{2,1,0:T(8,128)} %slice.119), channel_id=1, source_target_pairs={{0,8},{8,16},{16,24},{24,0},{1,9},{9,17},{17,25},{25,1},{2,10},{10... | collective-permute-start | bytes 3080 | tf_op jit(solution)/shard_map/ppermute | solution.py:11
  5.8 1.0 convert_element_type.6
  7.0 2.1 %copy_multiply_fusion = f32[4,4,64,256]{3,1,0,2:T(4,128)S(1)} fusion(f32[4,4,64,256]{3,2,1,0:T(8,128)} %param.12, f32[4,64,256]{2,0,1:T(4,128)S(1)} %copy.78), kind=kLoop, calls=%fused_computation.26 | loop fusion | flops 262144 | bytes 2359296 | tf_op jit(solution)/shard_map/mul | solution.py:48
  9.1 3.3 %collective-permute-start.5 = (f32[4,4,1,256]{3,1,0,2:T(4,128)S(1)}, f32[4,4,1,256]{3,1,0,2:T(4,128)S(1)}, u32[]{:S(2)}, u32[]{:S(2)}) collective-permute-start(f32[4,4,1,256]{3,1,0,2:T(4,128)S(1)} %get-tuple-element.38), channel_id=1, source_target_pairs={{0,1},{1,2},{2,3},{3,4},{4,5},{5,6},{6,7},{8,9},{9,10},{10,11},{11... | collective-permute-start | bytes 49160 | tf_op jit(solution)/shard_map/ppermute | solution.py:27
  12.4 2.3 %collective-permute-start.3 = (f32[4,4,1,256]{3,1,0,2:T(4,128)S(1)}, f32[4,4,1,256]{3,1,0,2:T(4,128)S(1)}, u32[]{:S(2)}, u32[]{:S(2)}) collective-permute-start(f32[4,4,1,256]{3,1,0,2:T(4,128)S(1)} %get-tuple-element.39), channel_id=1, source_target_pairs={{1,0},{2,1},{3,2},{4,3},{5,4},{6,5},{7,6},{9,8},{10,9},{11,10},{12... | collective-permute-start | bytes 49160 | tf_op jit(solution)/shard_map/ppermute | solution.py:30
  14.7 1.3 %fusion.26 = (f32[4,4,64,1]{3,1,0,2:T(4,128)}, f32[4,4,64,1]{3,1,0,2:T(4,128)}) fusion(f32[4,4,64,256]{3,1,0,2:T(4,128)S(1)} %copy_multiply_fusion), kind=kLoop, calls=%fused_computation.54 | loop fusion | bytes 16384 | tf_op jit(solution)/shard_map/slice | solution.py:28
  16.0 1.5 %collective-permute-start.2 = (f32[4,4,64,1]{3,1,0,2:T(4,128)}, f32[4,4,64,1]{3,1,0,2:T(4,128)}, u32[]{:S(2)}, u32[]{:S(2)}) collective-permute-start(f32[4,4,64,1]{3,1,0,2:T(4,128)} %get-tuple-element.42), channel_id=1, source_target_pairs={{0,8},{8,16},{16,24},{24,0},{1,9},{9,17},{17,25},{25,1},{2,10},{10... | collective-permute-start | bytes 12296 | tf_op jit(solution)/shard_map/ppermute | solution.py:27
  18.1 1.8 %fusion.25 = (f32[4,4,63,256]{3,1,0,2:T(4,128)}, f32[4,4,63,256]{3,1,0,2:T(4,128)}) fusion(f32[4,4,64,256]{3,1,0,2:T(4,128)S(1)} %copy_multiply_fusion), kind=kLoop, calls=%fused_computation.53 | loop fusion | bytes 4128768 | tf_op jit(solution)/shard_map/slice | solution.py:58
  19.9 1.7 %fusion.27 = (f32[4,4,64,255]{3,1,0,2:T(4,128)S(1)}, f32[4,4,64,255]{3,1,0,2:T(4,128)}) fusion(f32[4,4,64,256]{3,1,0,2:T(4,128)S(1)} %copy_multiply_fusion), kind=kLoop, calls=%fused_computation.55 | loop fusion | bytes 4177920 | tf_op jit(solution)/shard_map/slice | solution.py:56
  21.6 12.3 %all_gather.6 = f32[4,4,1024]{2,1,0:T(4,128)S(1)} all-gather(f32[4,4,256]{2,1,0:T(4,128)S(1)} %bitcast_multiply_fusion.3), channel_id=1, replica_groups=mesh['lon'=4,'lat'=8] {'lon'}, dimensions={2}, use_global_device_ids=true | all-gather | bytes 81920 | tf_op jit(solution)/shard_map/all_gather | solution.py:66
  33.9 0.9 copy.80
  34.8 0.9 copy.82
  35.7 1.7 %copy.84 = f32[4,4,1024]{1,0,2:T(4,128)} copy(f32[4,4,1024]{2,1,0:T(4,128)S(1)} %all_gather.6) | data formatting | bytes 131072 | tf_op jit(solution)/shard_map/all_gather | solution.py:66
  37.4 2.6 %gather_fusion = f32[256,4,4]{2,1,0:T(4,128)S(1)} fusion(f32[4,4,1024]{1,0,2:T(4,128)} %copy.84, s32[1024]{0:T(1024)S(1)} %pad_clamp_fusion), kind=kCustom, calls=%fused_computation.clone | custom fusion | bytes 33792 | tf_op jit(solution)/shard_map/jit(_take)/gather | solution.py:67
  40.6 1.0 maximum_multiply_fusion
  42.1 12.2 %collective-permute-done = f32[4,4,64,1]{3,1,0,2:T(4,128)S(1)} collective-permute-done((f32[4,4,64,1]{3,1,0,2:T(4,128)}, f32[4,4,64,1]{3,1,0,2:T(4,128)S(1)}, u32[]{:S(2)}, u32[]{:S(2)}) %collective-permute-start) | collective-permute-done | bytes 4128 | tf_op jit(solution)/shard_map/ppermute | solution.py:30
  54.4 4.6 %fusion.4 = f32[4,4,64,256]{3,1,0,2:T(4,128)S(1)} fusion(f32[4,4,64,1]{3,1,0,2:T(4,128)S(1)} %collective-permute-done, f32[4,4,64,255]{3,1,0,2:T(4,128)} %get-tuple-element.45, f32[4,4,64,255]{3,1,0,2:T(4,128)S(1)} %get-tuple-element.44, f32[4,4,64,1]{3,1,0,2:T(4,128)} %collective-permute-done.2, f32[4,4,1,256]{3,1,0,2:T(4,128)S(1)} %collective-permute-done.3, ...), kind=kLoop, calls=%fused_computation.7 | loop fusion | flops 4456448 | bytes 7602176 | tf_op jit(solution)/shard_map/add | solution.py:69
  59.5 1.4 %fusion.22 = (f32[4,4,64,1]{3,1,0,2:T(4,128)}, f32[4,4,64,1]{3,1,0,2:T(4,128)}) fusion(f32[4,4,64,256]{3,1,0,2:T(4,128)S(1)} %multiply_multiply_fusion), kind=kLoop, calls=%fused_computation.50 | loop fusion | bytes 16384 | tf_op jit(solution)/shard_map/slice | solution.py:28
  60.8 1.8 %fusion.21 = (f32[4,4,63,256]{3,1,0,2:T(4,128)}, f32[4,4,63,256]{3,1,0,2:T(4,128)}) fusion(f32[4,4,64,256]{3,1,0,2:T(4,128)S(1)} %multiply_multiply_fusion), kind=kLoop, calls=%fused_computation.49 | loop fusion | bytes 4128768 | tf_op jit(solution)/shard_map/slice | solution.py:58
  62.6 0.7 fusion.23
  63.4 1.9 %collective-permute-start.9 = (f32[4,4,1,256]{3,1,0,2:T(4,128)S(1)}, f32[4,4,1,256]{3,1,0,2:T(4,128)S(1)}, u32[]{:S(2)}, u32[]{:S(2)}) collective-permute-start(f32[4,4,1,256]{3,1,0,2:T(4,128)S(1)} %get-tuple-element.30), channel_id=1, source_target_pairs={{0,1},{1,2},{2,3},{3,4},{4,5},{5,6},{6,7},{8,9},{9,10},{10,11},{11... | collective-permute-start | bytes 49160 | tf_op jit(solution)/shard_map/ppermute | solution.py:27
  65.3 3.6 %collective-permute-start.8 = (f32[4,4,1,256]{3,1,0,2:T(4,128)S(1)}, f32[4,4,1,256]{3,1,0,2:T(4,128)S(1)}, u32[]{:S(2)}, u32[]{:S(2)}) collective-permute-start(f32[4,4,1,256]{3,1,0,2:T(4,128)S(1)} %get-tuple-element.31), channel_id=1, source_target_pairs={{1,0},{2,1},{3,2},{4,3},{5,4},{6,5},{7,6},{9,8},{10,9},{11,10},{12... | collective-permute-start | bytes 49160 | tf_op jit(solution)/shard_map/ppermute | solution.py:30
  69.4 1.7 %collective-permute-start.6 = (f32[4,4,64,1]{3,1,0,2:T(4,128)}, f32[4,4,64,1]{3,1,0,2:T(4,128)}, u32[]{:S(2)}, u32[]{:S(2)}) collective-permute-start(f32[4,4,64,1]{3,1,0,2:T(4,128)} %get-tuple-element.35), channel_id=1, source_target_pairs={{8,0},{16,8},{24,16},{0,24},{9,1},{17,9},{25,17},{1,25},{10,2},{18... | collective-permute-start | bytes 12296 | tf_op jit(solution)/shard_map/ppermute | solution.py:30
  71.0 25.6 %all_gather.7 = f32[4,4,1024]{2,1,0:T(4,128)S(1)} all-gather(f32[4,4,256]{2,1,0:T(4,128)S(1)} %bitcast_multiply_fusion.1), channel_id=1, replica_groups=mesh['lon'=4,'lat'=8] {'lon'}, dimensions={2}, use_global_device_ids=true | all-gather | bytes 81920 | tf_op jit(solution)/shard_map/all_gather | solution.py:66
  96.7 1.7 %copy.86 = f32[4,4,1024]{1,0,2:T(4,128)} copy(f32[4,4,1024]{2,1,0:T(4,128)S(1)} %all_gather.7) | data formatting | bytes 131072 | tf_op jit(solution)/shard_map/all_gather | solution.py:66
  98.4 3.4 %gather_fusion.1 = f32[256,4,4]{2,1,0:T(4,128)} fusion(f32[4,4,1024]{1,0,2:T(4,128)} %copy.86, s32[1024]{0:T(1024)S(1)} %pad_clamp_fusion), kind=kCustom, calls=%fused_computation.1.clone | custom fusion | bytes 33792 | tf_op jit(solution)/shard_map/jit(_take)/gather | solution.py:67
  101.7 1.2 %copy.87 = f32[256,4,4]{0,2,1:T(4,128)S(1)} copy(f32[256,4,4]{2,1,0:T(4,128)} %gather_fusion.1) | data formatting | bytes 32768 | tf_op jit(solution)/shard_map/jit(_take)/gather | solution.py:67
  103.0 4.1 %fusion.12 = f32[4,4,64,256]{3,1,0,2:T(4,128)S(1)} fusion(f32[4,4,64,1]{3,1,0,2:T(4,128)} %collective-permute-done.6, f32[4,4,64,255]{3,1,0,2:T(4,128)S(1)} %get-tuple-element.37, f32[4,4,64,255]{3,1,0,2:T(4,128)S(1)} %get-tuple-element.36, f32[4,4,64,1]{3,1,0,2:T(4,128)} %collective-permute-done.7, f32[4,4,1,256]{3,1,0,2:T(4,128)S(1)} %collective-permute-done.8, ...), kind=kLoop, calls=%fused_computation.19 | loop fusion | flops 4718592 | bytes 7602176 | tf_op jit(solution)/shard_map/add | solution.py:69
  107.5 1.6 %copy.88 = f32[4,4,64,256]{3,2,1,0:T(8,128)} copy(f32[4,4,64,256]{3,1,0,2:T(4,128)S(1)} %broadcast_multiply_fusion) | data formatting | bytes 2097152 | tf_op jit(solution)/shard_map/mul | solution.py:71
  (48 shorter events, 3.0 us)
Async XLA Ops:
  0.8 41.1 %collective-permute-start.4 = (f32[4,1,256]{2,1,0:T(1,128)S(1)}, f32[4,1,256]{2,1,0:T(1,128)S(1)}, u32[]{:S(2)}, u32[]{:S(2)}) collective-permute-start(f32[4,1,256]{2,1,0:T(1,128)S(1)} %get-tuple-element.47), channel_id=1, source_target_pairs={{0,1},{1,2},{2,3},{3,4},{4,5},{5,6},{6,7},{8,9},{9,10},{10,11},{11... | collective-permute-start | bytes 12296 | tf_op jit(solution)/shard_map/ppermute | solution.py:17
  4.3 35.8 %collective-permute-start.1 = (f32[4,64,1]{2,1,0:T(8,128)}, f32[4,64,1]{2,1,0:T(8,128)}, u32[]{:S(2)}, u32[]{:S(2)}) collective-permute-start(f32[4,64,1]{2,1,0:T(8,128)} %slice.119), channel_id=1, source_target_pairs={{0,8},{8,16},{16,24},{24,0},{1,9},{9,17},{17,25},{25,1},{2,10},{10... | collective-permute-start | bytes 3080 | tf_op jit(solution)/shard_map/ppermute | solution.py:11
  7.0 10.5 %copy-start.8 = (s32[256]{0:T(256)S(1)}, s32[256]{0:T(256)}, u32[]{:S(2)}) copy-start(s32[256]{0:T(256)} %param.16) | copy-start | bytes 3076
  7.0 11.0 %copy-start.4 = (f32[4,64,256]{2,1,0:T(8,128)S(1)}, f32[4,64,256]{2,1,0:T(8,128)}, u32[]{:S(2)}) copy-start(f32[4,64,256]{2,1,0:T(8,128)} %param.13) | copy-start | bytes 786436
  7.0 11.0 %copy-start.5 = (f32[4,64,256]{2,1,0:T(8,128)S(1)}, f32[4,64,256]{2,1,0:T(8,128)}, u32[]{:S(2)}) copy-start(f32[4,64,256]{2,1,0:T(8,128)} %param.14) | copy-start | bytes 786436
  9.1 45.2 %collective-permute-start.5 = (f32[4,4,1,256]{3,1,0,2:T(4,128)S(1)}, f32[4,4,1,256]{3,1,0,2:T(4,128)S(1)}, u32[]{:S(2)}, u32[]{:S(2)}) collective-permute-start(f32[4,4,1,256]{3,1,0,2:T(4,128)S(1)} %get-tuple-element.38), channel_id=1, source_target_pairs={{0,1},{1,2},{2,3},{3,4},{4,5},{5,6},{6,7},{8,9},{9,10},{10,11},{11... | collective-permute-start | bytes 49160 | tf_op jit(solution)/shard_map/ppermute | solution.py:27
  12.4 41.9 %collective-permute-start.3 = (f32[4,4,1,256]{3,1,0,2:T(4,128)S(1)}, f32[4,4,1,256]{3,1,0,2:T(4,128)S(1)}, u32[]{:S(2)}, u32[]{:S(2)}) collective-permute-start(f32[4,4,1,256]{3,1,0,2:T(4,128)S(1)} %get-tuple-element.39), channel_id=1, source_target_pairs={{1,0},{2,1},{3,2},{4,3},{5,4},{6,5},{7,6},{9,8},{10,9},{11,10},{12... | collective-permute-start | bytes 49160 | tf_op jit(solution)/shard_map/ppermute | solution.py:30
  16.0 26.0 %collective-permute-start.2 = (f32[4,4,64,1]{3,1,0,2:T(4,128)}, f32[4,4,64,1]{3,1,0,2:T(4,128)}, u32[]{:S(2)}, u32[]{:S(2)}) collective-permute-start(f32[4,4,64,1]{3,1,0,2:T(4,128)} %get-tuple-element.42), channel_id=1, source_target_pairs={{0,8},{8,16},{16,24},{24,0},{1,9},{9,17},{17,25},{25,1},{2,10},{10... | collective-permute-start | bytes 12296 | tf_op jit(solution)/shard_map/ppermute | solution.py:27
  35.7 18.7 %copy-start = (f32[4,4,64,256]{3,2,1,0:T(8,128)S(1)}, f32[4,4,64,256]{3,2,1,0:T(8,128)}, u32[]{:S(2)}) copy-start(f32[4,4,64,256]{3,2,1,0:T(8,128)} %param.12) | copy-start | bytes 3145732
  40.2 14.2 %copy-start.1 = (f32[4,64,256]{2,0,1:T(4,128)S(1)}, f32[4,64,256]{2,0,1:T(4,128)}, u32[]{:S(2)}) copy-start(f32[4,64,256]{2,0,1:T(4,128)} %copy.82) | copy-start | bytes 786436
  40.2 14.1 %collective-permute-start = (f32[4,4,64,1]{3,1,0,2:T(4,128)}, f32[4,4,64,1]{3,1,0,2:T(4,128)S(1)}, u32[]{:S(2)}, u32[]{:S(2)}) collective-permute-start(f32[4,4,64,1]{3,1,0,2:T(4,128)} %get-tuple-element.43), channel_id=1, source_target_pairs={{8,0},{16,8},{24,16},{0,24},{9,1},{17,9},{25,17},{1,25},{10,2},{18... | collective-permute-start | bytes 12296 | tf_op jit(solution)/shard_map/ppermute | solution.py:30
  41.8 17.2 %copy-start.2 = (f32[4,64,256]{2,0,1:T(4,128)}, f32[4,64,256]{2,0,1:T(4,128)S(1)}, u32[]{:S(2)}) copy-start(f32[4,64,256]{2,0,1:T(4,128)S(1)} %copy.81) | copy-start | bytes 786436
  42.1 17.0 %copy-start.3 = (f32[4,64,256]{2,0,1:T(4,128)}, f32[4,64,256]{2,0,1:T(4,128)S(1)}, u32[]{:S(2)}) copy-start(f32[4,64,256]{2,0,1:T(4,128)S(1)} %copy.83) | copy-start | bytes 786436
  54.3 4.7 %copy-start.6 = (f32[4]{0:T(128)S(1)}, f32[4]{0:T(128)}, u32[]{:S(2)}) copy-start(f32[4]{0:T(128)} %constant.73) | copy-start | bytes 52
  54.4 4.7 %copy-start.7 = (pred[256]{0:T(512)(128)(4,1)S(1)}, pred[256]{0:T(512)(128)(4,1)}, u32[]{:S(2)}) copy-start(pred[256]{0:T(512)(128)(4,1)} %compare_and_fusion) | copy-start | bytes 772
  63.4 39.6 %collective-permute-start.9 = (f32[4,4,1,256]{3,1,0,2:T(4,128)S(1)}, f32[4,4,1,256]{3,1,0,2:T(4,128)S(1)}, u32[]{:S(2)}, u32[]{:S(2)}) collective-permute-start(f32[4,4,1,256]{3,1,0,2:T(4,128)S(1)} %get-tuple-element.30), channel_id=1, source_target_pairs={{0,1},{1,2},{2,3},{3,4},{4,5},{5,6},{6,7},{8,9},{9,10},{10,11},{11... | collective-permute-start | bytes 49160 | tf_op jit(solution)/shard_map/ppermute | solution.py:27
  65.3 37.7 %collective-permute-start.8 = (f32[4,4,1,256]{3,1,0,2:T(4,128)S(1)}, f32[4,4,1,256]{3,1,0,2:T(4,128)S(1)}, u32[]{:S(2)}, u32[]{:S(2)}) collective-permute-start(f32[4,4,1,256]{3,1,0,2:T(4,128)S(1)} %get-tuple-element.31), channel_id=1, source_target_pairs={{1,0},{2,1},{3,2},{4,3},{5,4},{6,5},{7,6},{9,8},{10,9},{11,10},{12... | collective-permute-start | bytes 49160 | tf_op jit(solution)/shard_map/ppermute | solution.py:30
  69.0 34.0 %collective-permute-start.7 = (f32[4,4,64,1]{3,1,0,2:T(4,128)}, f32[4,4,64,1]{3,1,0,2:T(4,128)}, u32[]{:S(2)}, u32[]{:S(2)}) collective-permute-start(f32[4,4,64,1]{3,1,0,2:T(4,128)} %get-tuple-element.34), channel_id=1, source_target_pairs={{0,8},{8,16},{16,24},{24,0},{1,9},{9,17},{17,25},{25,1},{2,10},{10... | collective-permute-start | bytes 12296 | tf_op jit(solution)/shard_map/ppermute | solution.py:27
  69.4 33.6 %collective-permute-start.6 = (f32[4,4,64,1]{3,1,0,2:T(4,128)}, f32[4,4,64,1]{3,1,0,2:T(4,128)}, u32[]{:S(2)}, u32[]{:S(2)}) collective-permute-start(f32[4,4,64,1]{3,1,0,2:T(4,128)} %get-tuple-element.35), channel_id=1, source_target_pairs={{8,0},{16,8},{24,16},{0,24},{9,1},{17,9},{25,17},{1,25},{10,2},{18... | collective-permute-start | bytes 12296 | tf_op jit(solution)/shard_map/ppermute | solution.py:30
where the time goes:
time: 110 us; the launch traced here: 109 us
  blocking collectives  37.9 us (34%)
  local copies, waits for them, and re-layouts  25.1 us (23%)
  starting transfers between devices  18.5 us (17%)
  other arithmetic  14.9 us (14%)
  waiting for transfers between devices  12.3 us (11%)
    all_gather x2, blocking collectives, per_device(): whole_row = lax.all_gather(fold_flux, 'lon', axis=2, tiled=True)  37.9 us
    ppermute x4, waiting for transfers between devices, with_halo(): lax.ppermute(lax.slice_in_dim(block, 0, width, axis=dim), axis, backward)  12.2 us
    add x2, other arithmetic, per_device(): total = masked + transport  8.75 us
    ppermute x4, starting transfers between devices, with_halo(): lax.ppermute(lax.slice_in_dim(block, 0, width, axis=dim), axis, backward)  8 us
    gather x4, local copies, waits for them, and re-layouts, per_device(): picked = jnp.take(whole_row, partner, axis=2)  7.4 us
    ppermute x4, starting transfers between devices, with_halo(): lax.ppermute(lax.slice_in_dim(block, block.shape[dim] - width, None, axis...  7.11 us
    slice x2, local copies, waits for them, and re-layouts, per_device(): masked[:, :, :-1, :]  3.65 us
    all_gather x2, local copies, waits for them, and re-layouts, per_device(): whole_row = lax.all_gather(fold_flux, 'lon', axis=2, tiled=True)  3.41 us
  transfers between devices with their start and end apart: 10, of which 1 were waited for; matrix products, arithmetic and copies ran while one was open for 22% of the time, Pallas kernels for 0%

commit v1 on v0

--- a/solution.py
+++ b/solution.py
@@ -4,6 +4,23 @@
 from jax.sharding import PartitionSpec as P
 
 STEPS = 2
+
+
+def switch_goods_now(block_in):
+    mesh_name = "lon"
+    devs = lax.axis_size(mesh_name)
+    seen = []
+    p = 0
+    while p < devs:
+        seen.append((p, (p + 1) % devs))
+        p = p + 1
+    y = [None] * devs
+    y[devs - 1] = block_in
+    for kk in range(devs - 2, -1, -1):
+        y[kk] = lax.ppermute(y[kk + 1], mesh_name, seen)
+    moved = jnp.concatenate(y, axis=2)
+    frame_out = (lax.axis_index(mesh_name) + 1) * block_in.shape[2]
+    return jnp.roll(moved, frame_out, axis=2)
 
 
 def shifted(shard, axis, by):
@@ -63,7 +80,7 @@
             + 0.5 * south_speed * (masked - south_adj)
         )
         fold_flux = fold_weight * masked[:, :, -1, :]
-        whole_row = lax.all_gather(fold_flux, "lon", axis=2, tiled=True)
+        whole_row = switch_goods_now(fold_flux)
         picked = jnp.take(whole_row, partner, axis=2)
         folded = 0.5 * fold_signs * picked
         total = masked + transport

time: 110 us -> 109 us (level)
  blocking collectives: 37.9 us -> 0 us
  waiting for transfers between devices: 12.3 us -> 40.7 us
  starting transfers between devices: 18.5 us -> 30.4 us
  local copies, waits for them, and re-layouts: 25.1 us -> 20.1 us
  other arithmetic: 14.9 us -> 16.6 us
    ppermute x0 -> x6, waiting for transfers between devices: none -> 40.7 us  [switch_goods_now(): y[kk] = lax.ppermute(y[kk + 1], mesh_name, seen)]
    all_gather x2 -> x0, blocking collectives: 37.9 us -> none  [per_device(): whole_row = lax.all_gather(fold_flux, 'lon', axis=2, tiled=True)]
    ppermute x4, waiting for transfers between devices: 12.2 us -> 0.01 us  [with_halo(): lax.ppermute(lax.slice_in_dim(block, 0, width, axis=dim), axis, backward)]
    ppermute x0 -> x6, starting transfers between devices: none -> 11.2 us  [switch_goods_now(): y[kk] = lax.ppermute(y[kk + 1], mesh_name, seen)]
    all_gather x2 -> x0, local copies, waits for them, and re-layouts: 3.41 us -> none  [per_device(): whole_row = lax.all_gather(fold_flux, 'lon', axis=2, tiled=True)]
    unnamed x19 -> x39, local copies, waits for them, and re-layouts: 0.05 us -> 1.85 us
    add x2, other arithmetic: 8.75 us -> 7.08 us  [per_device(): total = masked + transport]
    slice x2, local copies, waits for them, and re-layouts: 3.65 us -> 2.14 us  [per_device(): masked[:, :, :-1, :]]
  transfers between devices with their start and end apart: 10 -> 16, of which waited for: 1 -> 2; matrix products, arithmetic and copies ran while one was open for 22% -> 21% of each run, Pallas kernels for 0% -> 0%
where the time goes in v1:
time: 109 us; the launch traced here: 108 us
  waiting for transfers between devices  40.7 us (37%)
  starting transfers between devices  30.4 us (28%)
  local copies, waits for them, and re-layouts  20.1 us (18%)
  other arithmetic  16.6 us (15%)
    ppermute x6, waiting for transfers between devices, switch_goods_now(): y[kk] = lax.ppermute(y[kk + 1], mesh_name, seen)  40.7 us
    ppermute x6, starting transfers between devices, switch_goods_now(): y[kk] = lax.ppermute(y[kk + 1], mesh_name, seen)  11.2 us
    ppermute x4, starting transfers between devices, with_halo(): lax.ppermute(lax.slice_in_dim(block, block.shape[dim] - width, None, axis...  7.9 us
    ppermute x4, starting transfers between devices, with_halo(): lax.ppermute(lax.slice_in_dim(block, 0, width, axis=dim), axis, backward)  7.78 us
    add x2, other arithmetic, per_device(): total = masked + transport  7.08 us
    gather x4, local copies, waits for them, and re-layouts, per_device(): picked = jnp.take(whole_row, partner, axis=2)  5.96 us
    slice x2, local copies, waits for them, and re-layouts, per_device(): west_adj = jnp.concatenate([west_rim[..., None], masked[..., :-1]], axis=3)  2.4 us
    mul x2, other arithmetic, per_device(): masked = wet_cells * current  2.31 us
  transfers between devices with their start and end apart: 16, of which 2 were waited for; matrix products, arithmetic and copies ran while one was open for 21% of the time, Pallas kernels for 0%

profile of v1, /device:TPU:10, one launch (start us, length us, event | category | flops | bytes accessed | tf_op | source)
XLA Modules:
  0.0 108.2 jit_solution(12728100343864229655)
XLA Ops:
  0.0 1.4 %broadcast_add_fusion = (f32[4,1,256]{2,1,0:T(1,128)S(1)}, f32[4,1,256]{2,1,0:T(1,128)}) fusion(f32[4,64,256]{2,1,0:T(8,128)} %param.16), kind=kLoop, calls=%fused_computation.76 | loop fusion | flops 1024 | bytes 12288 | tf_op jit(solution)/shard_map/add | solution.py:62
  1.4 2.0 %collective-permute-start.4 = (f32[4,1,256]{2,1,0:T(1,128)}, f32[4,1,256]{2,1,0:T(1,128)}, u32[]{:S(2)}, u32[]{:S(2)}) collective-permute-start(f32[4,1,256]{2,1,0:T(1,128)} %get-tuple-element.48), channel_id=1, source_target_pairs={{0,1},{1,2},{2,3},{3,4},{4,5},{5,6},{6,7},{8,9},{9,10},{10,11},{11... | collective-permute-start | bytes 12296 | tf_op jit(solution)/shard_map/ppermute | solution.py:34
  3.5 1.7 %slice.119 = f32[4,64,1]{2,1,0:T(8,128)} slice(f32[4,64,256]{2,1,0:T(8,128)} %param.15), slice={[0:4], [0:64], [255:256]} | slice | bytes 2048 | tf_op jit(solution)/shard_map/slice | solution.py:58
  5.1 1.5 %collective-permute-start.1 = (f32[4,64,1]{2,1,0:T(8,128)}, f32[4,64,1]{2,1,0:T(8,128)S(1)}, u32[]{:S(2)}, u32[]{:S(2)}) collective-permute-start(f32[4,64,1]{2,1,0:T(8,128)} %slice.119), channel_id=1, source_target_pairs={{0,8},{8,16},{16,24},{24,0},{1,9},{9,17},{17,25},{25,1},{2,10},{10... | collective-permute-start | bytes 3080 | tf_op jit(solution)/shard_map/ppermute | solution.py:28
  6.6 1.0 convert_element_type.6
  7.8 2.0 %copy_multiply_fusion = f32[4,4,64,256]{3,1,0,2:T(4,128)S(1)} fusion(f32[4,4,64,256]{3,2,1,0:T(8,128)} %param.14, f32[4,64,256]{2,0,1:T(4,128)S(1)} %copy.90), kind=kLoop, calls=%fused_computation.26 | loop fusion | flops 262144 | bytes 2359296 | tf_op jit(solution)/shard_map/mul | solution.py:65
  9.8 1.5 %collective-permute-start.6 = (f32[4,4,256]{2,1,0:T(4,128)S(1)}, f32[4,4,256]{2,1,0:T(4,128)}, u32[]{:S(2)}, u32[]{:S(2)}) collective-permute-start(f32[4,4,256]{2,1,0:T(4,128)S(1)} %bitcast_multiply_fusion.3), channel_id=1, source_target_pairs={{0,8},{8,16},{16,24},{24,0},{1,9},{9,17},{17,25},{25,1},{2,10},{10... | collective-permute-start | bytes 49160 | tf_op jit(solution)/shard_map/ppermute | solution.py:20
  12.0 3.0 %collective-permute-start.5 = (f32[4,4,1,256]{3,1,0,2:T(4,128)}, f32[4,4,1,256]{3,1,0,2:T(4,128)}, u32[]{:S(2)}, u32[]{:S(2)}) collective-permute-start(f32[4,4,1,256]{3,1,0,2:T(4,128)} %get-tuple-element.39), channel_id=1, source_target_pairs={{0,1},{1,2},{2,3},{3,4},{4,5},{5,6},{6,7},{8,9},{9,10},{10,11},{11... | collective-permute-start | bytes 49160 | tf_op jit(solution)/shard_map/ppermute | solution.py:44
  15.0 2.5 %collective-permute-start.3 = (f32[4,4,1,256]{3,1,0,2:T(4,128)}, f32[4,4,1,256]{3,1,0,2:T(4,128)}, u32[]{:S(2)}, u32[]{:S(2)}) collective-permute-start(f32[4,4,1,256]{3,1,0,2:T(4,128)} %get-tuple-element.40), channel_id=1, source_target_pairs={{1,0},{2,1},{3,2},{4,3},{5,4},{6,5},{7,6},{9,8},{10,9},{11,10},{12... | collective-permute-start | bytes 49160 | tf_op jit(solution)/shard_map/ppermute | solution.py:47
  18.7 1.3 %fusion.40 = (f32[4,4,64,1]{3,1,0,2:T(4,128)}, f32[4,4,64,1]{3,1,0,2:T(4,128)}) fusion(f32[4,4,64,256]{3,1,0,2:T(4,128)S(1)} %copy_multiply_fusion), kind=kLoop, calls=%fused_computation.84 | loop fusion | bytes 16384 | tf_op jit(solution)/shard_map/slice | solution.py:45
  20.1 1.9 %fusion.39 = (f32[4,4,63,256]{3,1,0,2:T(4,128)}, f32[4,4,63,256]{3,1,0,2:T(4,128)}) fusion(f32[4,4,64,256]{3,1,0,2:T(4,128)S(1)} %copy_multiply_fusion), kind=kLoop, calls=%fused_computation.83 | loop fusion | bytes 4128768 | tf_op jit(solution)/shard_map/slice | solution.py:75
  21.9 1.7 %fusion.41 = (f32[4,4,64,255]{3,1,0,2:T(4,128)S(1)}, f32[4,4,64,255]{3,1,0,2:T(4,128)}) fusion(f32[4,4,64,256]{3,1,0,2:T(4,128)S(1)} %copy_multiply_fusion), kind=kLoop, calls=%fused_computation.85 | loop fusion | bytes 4177920 | tf_op jit(solution)/shard_map/slice | solution.py:73
  23.6 1.4 %pad_clamp_fusion = s32[1024]{0:T(1024)} fusion(s32[256]{0:T(256)} %compare_select_fusion), kind=kLoop, calls=%fused_computation.73 | loop fusion | flops 1024 | bytes 5120 | tf_op gather
  27.6 1.6 %collective-permute-start = (f32[4,4,64,1]{3,1,0,2:T(4,128)}, f32[4,4,64,1]{3,1,0,2:T(4,128)S(1)}, u32[]{:S(2)}, u32[]{:S(2)}) collective-permute-start(f32[4,4,64,1]{3,1,0,2:T(4,128)} %get-tuple-element.44), channel_id=1, source_target_pairs={{8,0},{16,8},{24,16},{0,24},{9,1},{17,9},{25,17},{1,25},{10,2},{18... | collective-permute-start | bytes 12296 | tf_op jit(solution)/shard_map/ppermute | solution.py:47
  29.2 1.4 %collective-permute-start.7 = (f32[4,4,256]{2,1,0:T(4,128)}, f32[4,4,256]{2,1,0:T(4,128)S(1)}, u32[]{:S(2)}, u32[]{:S(2)}) collective-permute-start(f32[4,4,256]{2,1,0:T(4,128)} %collective-permute-done.6), channel_id=1, source_target_pairs={{0,8},{8,16},{16,24},{24,0},{1,9},{9,17},{17,25},{25,1},{2,10},{10... | collective-permute-start | bytes 49160 | tf_op jit(solution)/shard_map/ppermute | solution.py:20
  31.5 20.9 %collective-permute-done.7 = f32[4,4,256]{2,1,0:T(4,128)S(1)} collective-permute-done((f32[4,4,256]{2,1,0:T(4,128)}, f32[4,4,256]{2,1,0:T(4,128)S(1)}, u32[]{:S(2)}, u32[]{:S(2)}) %collective-permute-start.7) | collective-permute-done | bytes 16416 | tf_op jit(solution)/shard_map/ppermute | solution.py:20
  52.3 1.4 %collective-permute-start.8 = (f32[4,4,256]{2,1,0:T(4,128)S(1)}, f32[4,4,256]{2,1,0:T(4,128)S(1)}, u32[]{:S(2)}, u32[]{:S(2)}) collective-permute-start(f32[4,4,256]{2,1,0:T(4,128)S(1)} %collective-permute-done.7), channel_id=1, source_target_pairs={{0,8},{8,16},{16,24},{24,0},{1,9},{9,17},{17,25},{25,1},{2,10},{10... | collective-permute-start | bytes 49160 | tf_op jit(solution)/shard_map/ppermute | solution.py:20
  53.8 4.3 %fusion.4 = f32[4,4,64,256]{3,1,0,2:T(4,128)S(1)} fusion(f32[4,4,64,1]{3,1,0,2:T(4,128)S(1)} %collective-permute-done, f32[4,4,64,255]{3,1,0,2:T(4,128)S(1)} %copy-done.1, f32[4,4,64,255]{3,1,0,2:T(4,128)S(1)} %get-tuple-element.45, f32[4,4,64,1]{3,1,0,2:T(4,128)S(1)} %collective-permute-done.2, f32[4,4,1,256]{3,1,0,2:T(4,128)} %collective-permute-done.3, ...), kind=kLoop, calls=%fused_computation.7 | loop fusion | flops 4456448 | bytes 7602176 | tf_op jit(solution)/shard_map/add | solution.py:86
  59.0 0.9 copy.102
  60.0 1.8 %gather_fusion = f32[256,4,4]{2,1,0:T(4,128)} fusion(f32[4,4,1024]{1,0,2:T(4,128)S(1)} %copy.102, s32[1024]{0:T(1024)S(1)} %copy-done.14), kind=kCustom, calls=%fused_computation.clone | custom fusion | bytes 33792 | tf_op jit(solution)/shard_map/jit(_take)/gather | solution.py:84
  61.7 1.2 %copy.97 = f32[256,4,4]{0,2,1:T(4,128)S(1)} copy(f32[256,4,4]{2,1,0:T(4,128)} %gather_fusion) | data formatting | bytes 32768 | tf_op jit(solution)/shard_map/jit(_take)/gather | solution.py:84
  65.1 1.9 %collective-permute-start.12 = (f32[4,4,1,256]{3,1,0,2:T(4,128)S(1)}, f32[4,4,1,256]{3,1,0,2:T(4,128)S(1)}, u32[]{:S(2)}, u32[]{:S(2)}) collective-permute-start(f32[4,4,1,256]{3,1,0,2:T(4,128)S(1)} %get-tuple-element.31), channel_id=1, source_target_pairs={{0,1},{1,2},{2,3},{3,4},{4,5},{5,6},{6,7},{8,9},{9,10},{10,11},{11... | collective-permute-start | bytes 49160 | tf_op jit(solution)/shard_map/ppermute | solution.py:44
  67.0 3.6 %collective-permute-start.11 = (f32[4,4,1,256]{3,1,0,2:T(4,128)S(1)}, f32[4,4,1,256]{3,1,0,2:T(4,128)S(1)}, u32[]{:S(2)}, u32[]{:S(2)}) collective-permute-start(f32[4,4,1,256]{3,1,0,2:T(4,128)S(1)} %get-tuple-element.32), channel_id=1, source_target_pairs={{1,0},{2,1},{3,2},{4,3},{5,4},{6,5},{7,6},{9,8},{10,9},{11,10},{12... | collective-permute-start | bytes 49160 | tf_op jit(solution)/shard_map/ppermute | solution.py:47
  70.7 2.4 %collective-permute-start.10 = (f32[4,4,64,1]{3,1,0,2:T(4,128)S(1)}, f32[4,4,64,1]{3,1,0,2:T(4,128)S(1)}, u32[]{:S(2)}, u32[]{:S(2)}) collective-permute-start(f32[4,4,64,1]{3,1,0,2:T(4,128)S(1)} %get-tuple-element.35), channel_id=1, source_target_pairs={{0,8},{8,16},{16,24},{24,0},{1,9},{9,17},{17,25},{25,1},{2,10},{10... | collective-permute-start | bytes 12296 | tf_op jit(solution)/shard_map/ppermute | solution.py:44
  73.1 2.9 %collective-permute-start.14 = (f32[4,4,256]{2,1,0:T(4,128)S(1)}, f32[4,4,256]{2,1,0:T(4,128)S(1)}, u32[]{:S(2)}, u32[]{:S(2)}) collective-permute-start(f32[4,4,256]{2,1,0:T(4,128)S(1)} %collective-permute-done.13), channel_id=1, source_target_pairs={{0,8},{8,16},{16,24},{24,0},{1,9},{9,17},{17,25},{25,1},{2,10},{10... | collective-permute-start | bytes 49160 | tf_op jit(solution)/shard_map/ppermute | solution.py:20
  76.3 19.8 %collective-permute-done.14 = f32[4,4,256]{2,1,0:T(4,128)S(1)} collective-permute-done((f32[4,4,256]{2,1,0:T(4,128)S(1)}, f32[4,4,256]{2,1,0:T(4,128)S(1)}, u32[]{:S(2)}, u32[]{:S(2)}) %collective-permute-start.14) | collective-permute-done | bytes 16416 | tf_op jit(solution)/shard_map/ppermute | solution.py:20
  96.1 3.3 %collective-permute-start.15 = (f32[4,4,256]{2,1,0:T(4,128)S(1)}, f32[4,4,256]{2,1,0:T(4,128)S(1)}, u32[]{:S(2)}, u32[]{:S(2)}) collective-permute-start(f32[4,4,256]{2,1,0:T(4,128)S(1)} %collective-permute-done.14), channel_id=1, source_target_pairs={{0,8},{8,16},{16,24},{24,0},{1,9},{9,17},{17,25},{25,1},{2,10},{10... | collective-permute-start | bytes 49160 | tf_op jit(solution)/shard_map/ppermute | solution.py:20
  99.5 2.7 %fusion.12 = f32[4,4,64,256]{3,1,0,2:T(4,128)S(1)} fusion(f32[4,4,64,1]{3,1,0,2:T(4,128)S(1)} %collective-permute-done.9, f32[4,4,64,255]{3,1,0,2:T(4,128)S(1)} %get-tuple-element.38, f32[4,4,64,255]{3,1,0,2:T(4,128)S(1)} %get-tuple-element.37, f32[4,4,64,1]{3,1,0,2:T(4,128)S(1)} %collective-permute-done.10, ...), kind=kLoop, calls=%fused_computation.19 | loop fusion | flops 4718592 | bytes 7602176 | tf_op jit(solution)/shard_map/add | solution.py:86
  102.4 0.9 copy.103
  103.3 1.8 %gather_fusion.1 = f32[256,4,4]{2,1,0:T(4,128)} fusion(f32[4,4,1024]{1,0,2:T(4,128)S(1)} %copy.103, s32[1024]{0:T(1024)S(1)} %copy-done.14), kind=kCustom, calls=%fused_computation.1.clone | custom fusion | bytes 33792 | tf_op jit(solution)/shard_map/jit(_take)/gather | solution.py:84
  105.0 1.2 %copy.99 = f32[256,4,4]{0,2,1:T(4,128)S(1)} copy(f32[256,4,4]{2,1,0:T(4,128)} %gather_fusion.1) | data formatting | bytes 32768 | tf_op jit(solution)/shard_map/jit(_take)/gather | solution.py:84
  106.6 1.6 %copy.100 = f32[4,4,64,256]{3,2,1,0:T(8,128)} copy(f32[4,4,64,256]{3,1,0,2:T(4,128)S(1)} %broadcast_multiply_fusion) | data formatting | bytes 2097152 | tf_op jit(solution)/shard_map/mul | solution.py:88
  (78 shorter events, 9.2 us)
Async XLA Ops:
  0.0 18.7 %copy-start.10 = (f32[4,64,256]{2,1,0:T(8,128)S(1)}, f32[4,64,256]{2,1,0:T(8,128)}, u32[]{:S(2)}) copy-start(f32[4,64,256]{2,1,0:T(8,128)} %param.15) | copy-start | bytes 786436
  0.0 17.5 %copy-start.17 = (s32[256]{0:T(256)S(1)}, s32[256]{0:T(256)}, u32[]{:S(2)}) copy-start(s32[256]{0:T(256)} %param.18) | copy-start | bytes 3076
  1.4 17.3 %copy-start.11 = (f32[4,64,256]{2,1,0:T(8,128)S(1)}, f32[4,64,256]{2,1,0:T(8,128)}, u32[]{:S(2)}) copy-start(f32[4,64,256]{2,1,0:T(8,128)} %param.16) | copy-start | bytes 786436
  1.4 26.2 %collective-permute-start.4 = (f32[4,1,256]{2,1,0:T(1,128)}, f32[4,1,256]{2,1,0:T(1,128)}, u32[]{:S(2)}, u32[]{:S(2)}) collective-permute-start(f32[4,1,256]{2,1,0:T(1,128)} %get-tuple-element.48), channel_id=1, source_target_pairs={{0,1},{1,2},{2,3},{3,4},{4,5},{5,6},{6,7},{8,9},{9,10},{10,11},{11... | collective-permute-start | bytes 12296 | tf_op jit(solution)/shard_map/ppermute | solution.py:34
  5.1 21.6 %collective-permute-start.1 = (f32[4,64,1]{2,1,0:T(8,128)}, f32[4,64,1]{2,1,0:T(8,128)S(1)}, u32[]{:S(2)}, u32[]{:S(2)}) collective-permute-start(f32[4,64,1]{2,1,0:T(8,128)} %slice.119), channel_id=1, source_target_pairs={{0,8},{8,16},{16,24},{24,0},{1,9},{9,17},{17,25},{25,1},{2,10},{10... | collective-permute-start | bytes 3080 | tf_op jit(solution)/shard_map/ppermute | solution.py:28
  6.6 12.0 %copy-start.12 = (f32[4,1,256]{2,0,1:T(4,128)}, f32[4,1,256]{2,0,1:T(4,128)S(1)}, u32[]{:S(2)}) copy-start(f32[4,1,256]{2,0,1:T(4,128)S(1)} %copy.108) | copy-start | bytes 12292
  9.8 19.4 %collective-permute-start.6 = (f32[4,4,256]{2,1,0:T(4,128)S(1)}, f32[4,4,256]{2,1,0:T(4,128)}, u32[]{:S(2)}, u32[]{:S(2)}) collective-permute-start(f32[4,4,256]{2,1,0:T(4,128)S(1)} %bitcast_multiply_fusion.3), channel_id=1, source_target_pairs={{0,8},{8,16},{16,24},{24,0},{1,9},{9,17},{17,25},{25,1},{2,10},{10... | collective-permute-start | bytes 49160 | tf_op jit(solution)/shard_map/ppermute | solution.py:20
  12.0 41.8 %collective-permute-start.5 = (f32[4,4,1,256]{3,1,0,2:T(4,128)}, f32[4,4,1,256]{3,1,0,2:T(4,128)}, u32[]{:S(2)}, u32[]{:S(2)}) collective-permute-start(f32[4,4,1,256]{3,1,0,2:T(4,128)} %get-tuple-element.39), channel_id=1, source_target_pairs={{0,1},{1,2},{2,3},{3,4},{4,5},{5,6},{6,7},{8,9},{9,10},{10,11},{11... | collective-permute-start | bytes 49160 | tf_op jit(solution)/shard_map/ppermute | solution.py:44
  15.0 38.8 %collective-permute-start.3 = (f32[4,4,1,256]{3,1,0,2:T(4,128)}, f32[4,4,1,256]{3,1,0,2:T(4,128)}, u32[]{:S(2)}, u32[]{:S(2)}) collective-permute-start(f32[4,4,1,256]{3,1,0,2:T(4,128)} %get-tuple-element.40), channel_id=1, source_target_pairs={{1,0},{2,1},{3,2},{4,3},{5,4},{6,5},{7,6},{9,8},{10,9},{11,10},{12... | collective-permute-start | bytes 49160 | tf_op jit(solution)/shard_map/ppermute | solution.py:47
  23.6 30.1 %copy-start = (f32[4,4,64,256]{3,2,1,0:T(8,128)S(1)}, f32[4,4,64,256]{3,2,1,0:T(8,128)}, u32[]{:S(2)}) copy-start(f32[4,4,64,256]{3,2,1,0:T(8,128)} %param.14) | copy-start | bytes 3145732
  26.7 27.1 %copy-start.1 = (f32[4,4,64,255]{3,1,0,2:T(4,128)S(1)}, f32[4,4,64,255]{3,1,0,2:T(4,128)}, u32[]{:S(2)}) copy-start(f32[4,4,64,255]{3,1,0,2:T(4,128)} %get-tuple-element.46) | copy-start | bytes 3133444
  26.7 27.1 %copy-start.2 = (f32[4,64,256]{2,0,1:T(4,128)S(1)}, f32[4,64,256]{2,0,1:T(4,128)}, u32[]{:S(2)}) copy-start(f32[4,64,256]{2,0,1:T(4,128)} %copy.92) | copy-start | bytes 786436
  26.7 27.1 %copy-start.4 = (f32[4,64,256]{2,0,1:T(4,128)S(1)}, f32[4,64,256]{2,0,1:T(4,128)}, u32[]{:S(2)}) copy-start(f32[4,64,256]{2,0,1:T(4,128)} %copy.94) | copy-start | bytes 786436
  26.7 27.0 %collective-permute-start.2 = (f32[4,4,64,1]{3,1,0,2:T(4,128)}, f32[4,4,64,1]{3,1,0,2:T(4,128)S(1)}, u32[]{:S(2)}, u32[]{:S(2)}) collective-permute-start(f32[4,4,64,1]{3,1,0,2:T(4,128)} %get-tuple-element.43), channel_id=1, source_target_pairs={{0,8},{8,16},{16,24},{24,0},{1,9},{9,17},{17,25},{25,1},{2,10},{10... | collective-permute-start | bytes 12296 | tf_op jit(solution)/shard_map/ppermute | solution.py:44
  27.6 30.6 %copy-start.6 = (f32[4,64,256]{2,0,1:T(4,128)}, f32[4,64,256]{2,0,1:T(4,128)S(1)}, u32[]{:S(2)}) copy-start(f32[4,64,256]{2,0,1:T(4,128)S(1)} %copy.93) | copy-start | bytes 786436
  27.6 26.2 %collective-permute-start = (f32[4,4,64,1]{3,1,0,2:T(4,128)}, f32[4,4,64,1]{3,1,0,2:T(4,128)S(1)}, u32[]{:S(2)}, u32[]{:S(2)}) collective-permute-start(f32[4,4,64,1]{3,1,0,2:T(4,128)} %get-tuple-element.44), channel_id=1, source_target_pairs={{8,0},{16,8},{24,16},{0,24},{9,1},{17,9},{25,17},{1,25},{10,2},{18... | collective-permute-start | bytes 12296 | tf_op jit(solution)/shard_map/ppermute | solution.py:47
  29.2 23.2 %collective-permute-start.7 = (f32[4,4,256]{2,1,0:T(4,128)}, f32[4,4,256]{2,1,0:T(4,128)S(1)}, u32[]{:S(2)}, u32[]{:S(2)}) collective-permute-start(f32[4,4,256]{2,1,0:T(4,128)} %collective-permute-done.6), channel_id=1, source_target_pairs={{0,8},{8,16},{16,24},{24,0},{1,9},{9,17},{17,25},{25,1},{2,10},{10... | collective-permute-start | bytes 49160 | tf_op jit(solution)/shard_map/ppermute | solution.py:20
  31.5 26.7 %copy-start.8 = (f32[4,64,256]{2,0,1:T(4,128)}, f32[4,64,256]{2,0,1:T(4,128)S(1)}, u32[]{:S(2)}) copy-start(f32[4,64,256]{2,0,1:T(4,128)S(1)} %copy.95) | copy-start | bytes 786436
  52.3 5.8 %collective-permute-start.8 = (f32[4,4,256]{2,1,0:T(4,128)S(1)}, f32[4,4,256]{2,1,0:T(4,128)S(1)}, u32[]{:S(2)}, u32[]{:S(2)}) collective-permute-start(f32[4,4,256]{2,1,0:T(4,128)S(1)} %collective-permute-done.7), channel_id=1, source_target_pairs={{0,8},{8,16},{16,24},{24,0},{1,9},{9,17},{17,25},{25,1},{2,10},{10... | collective-permute-start | bytes 49160 | tf_op jit(solution)/shard_map/ppermute | solution.py:20
  58.2 4.8 %copy-start.15 = (f32[4]{0:T(128)S(1)}, f32[4]{0:T(128)}, u32[]{:S(2)}) copy-start(f32[4]{0:T(128)} %constant.98) | copy-start | bytes 52
  58.2 4.8 %copy-start.16 = (pred[256]{0:T(512)(128)(4,1)S(1)}, pred[256]{0:T(512)(128)(4,1)}, u32[]{:S(2)}) copy-start(pred[256]{0:T(512)(128)(4,1)} %compare_and_fusion) | copy-start | bytes 772
  64.4 35.0 %copy-start.3 = (f32[4,64,256]{2,0,1:T(4,128)S(1)}, f32[4,64,256]{2,0,1:T(4,128)}, u32[]{:S(2)}) copy-start(f32[4,64,256]{2,0,1:T(4,128)} %copy.92) | copy-start | bytes 786436
  64.4 35.0 %copy-start.5 = (f32[4,64,256]{2,0,1:T(4,128)S(1)}, f32[4,64,256]{2,0,1:T(4,128)}, u32[]{:S(2)}) copy-start(f32[4,64,256]{2,0,1:T(4,128)} %copy.94) | copy-start | bytes 786436
  64.5 35.0 %copy-start.7 = (f32[4,64,256]{2,0,1:T(4,128)S(1)}, f32[4,64,256]{2,0,1:T(4,128)}, u32[]{:S(2)}) copy-start(f32[4,64,256]{2,0,1:T(4,128)} %copy-done.6) | copy-start | bytes 786436
  64.5 35.0 %copy-start.9 = (f32[4,64,256]{2,0,1:T(4,128)S(1)}, f32[4,64,256]{2,0,1:T(4,128)}, u32[]{:S(2)}) copy-start(f32[4,64,256]{2,0,1:T(4,128)} %copy-done.8) | copy-start | bytes 786436
  64.5 8.7 %collective-permute-start.13 = (f32[4,4,256]{2,1,0:T(4,128)S(1)}, f32[4,4,256]{2,1,0:T(4,128)S(1)}, u32[]{:S(2)}, u32[]{:S(2)}) collective-permute-start(f32[4,4,256]{2,1,0:T(4,128)S(1)} %bitcast_multiply_fusion.1), channel_id=1, source_target_pairs={{0,8},{8,16},{16,24},{24,0},{1,9},{9,17},{17,25},{25,1},{2,10},{10... | collective-permute-start | bytes 49160 | tf_op jit(solution)/shard_map/ppermute | solution.py:20
  65.1 34.3 %collective-permute-start.12 = (f32[4,4,1,256]{3,1,0,2:T(4,128)S(1)}, f32[4,4,1,256]{3,1,0,2:T(4,128)S(1)}, u32[]{:S(2)}, u32[]{:S(2)}) collective-permute-start(f32[4,4,1,256]{3,1,0,2:T(4,128)S(1)} %get-tuple-element.31), channel_id=1, source_target_pairs={{0,1},{1,2},{2,3},{3,4},{4,5},{5,6},{6,7},{8,9},{9,10},{10,11},{11... | collective-permute-start | bytes 49160 | tf_op jit(solution)/shard_map/ppermute | solution.py:44
  67.0 32.4 %collective-permute-start.11 = (f32[4,4,1,256]{3,1,0,2:T(4,128)S(1)}, f32[4,4,1,256]{3,1,0,2:T(4,128)S(1)}, u32[]{:S(2)}, u32[]{:S(2)}) collective-permute-start(f32[4,4,1,256]{3,1,0,2:T(4,128)S(1)} %get-tuple-element.32), channel_id=1, source_target_pairs={{1,0},{2,1},{3,2},{4,3},{5,4},{6,5},{7,6},{9,8},{10,9},{11,10},{12... | collective-permute-start | bytes 49160 | tf_op jit(solution)/shard_map/ppermute | solution.py:47
  70.7 28.7 %collective-permute-start.10 = (f32[4,4,64,1]{3,1,0,2:T(4,128)S(1)}, f32[4,4,64,1]{3,1,0,2:T(4,128)S(1)}, u32[]{:S(2)}, u32[]{:S(2)}) collective-permute-start(f32[4,4,64,1]{3,1,0,2:T(4,128)S(1)} %get-tuple-element.35), channel_id=1, source_target_pairs={{0,8},{8,16},{16,24},{24,0},{1,9},{9,17},{17,25},{25,1},{2,10},{10... | collective-permute-start | bytes 12296 | tf_op jit(solution)/shard_map/ppermute | solution.py:44
  73.1 26.3 %collective-permute-start.9 = (f32[4,4,64,1]{3,1,0,2:T(4,128)S(1)}, f32[4,4,64,1]{3,1,0,2:T(4,128)S(1)}, u32[]{:S(2)}, u32[]{:S(2)}) collective-permute-start(f32[4,4,64,1]{3,1,0,2:T(4,128)S(1)} %get-tuple-element.36), channel_id=1, source_target_pairs={{8,0},{16,8},{24,16},{0,24},{9,1},{17,9},{25,17},{1,25},{10,2},{18... | collective-permute-start | bytes 12296 | tf_op jit(solution)/shard_map/ppermute | solution.py:47
  73.1 23.0 %collective-permute-start.14 = (f32[4,4,256]{2,1,0:T(4,128)S(1)}, f32[4,4,256]{2,1,0:T(4,128)S(1)}, u32[]{:S(2)}, u32[]{:S(2)}) collective-permute-start(f32[4,4,256]{2,1,0:T(4,128)S(1)} %collective-permute-done.13), channel_id=1, source_target_pairs={{0,8},{8,16},{16,24},{24,0},{1,9},{9,17},{17,25},{25,1},{2,10},{10... | collective-permute-start | bytes 49160 | tf_op jit(solution)/shard_map/ppermute | solution.py:20
  96.1 6.1 %collective-permute-start.15 = (f32[4,4,256]{2,1,0:T(4,128)S(1)}, f32[4,4,256]{2,1,0:T(4,128)S(1)}, u32[]{:S(2)}, u32[]{:S(2)}) collective-permute-start(f32[4,4,256]{2,1,0:T(4,128)S(1)} %collective-permute-done.14), channel_id=1, source_target_pairs={{0,8},{8,16},{16,24},{24,0},{1,9},{9,17},{17,25},{25,1},{2,10},{10... | collective-permute-start | bytes 49160 | tf_op jit(solution)/shard_map/ppermute | solution.py:20
  (2 other events, 6.1 us)
